TPU v7x, 32 devices: a whole 2x2x4 slice. The times are simulated.
32 devices in a mesh: ctx: 4 (over y, x), fsdp: 8 (over z, core).
Axes of the slice: x: 2, y: 2, z: 4, core: 2. Of those that a mesh axis runs over, the one named last changes fastest.
Arguments:
- tokens: bfloat16 [2, 8, 1024, 1024], P(None, 'fsdp', 'ctx'), may hold values from -6 to 6
- doc_lengths: int32 [2, 8, 4], P(None, 'fsdp'), may hold values from 1 to 512, 1024 in all within a row
- w_query: bfloat16 [1024, 1024], P(('ctx', 'fsdp')), may hold values from -0.1875 to 0.1875
- b_query: bfloat16 [1024], P(('ctx', 'fsdp')), may hold values from -1.75 to 1.75
- w_key: bfloat16 [1024, 1024], P(('ctx', 'fsdp')), may hold values from -0.1875 to 0.1875
- w_value: bfloat16 [1024, 1024], P(('ctx', 'fsdp')), may hold values from -0.1875 to 0.1875
- b_value: bfloat16 [1024], P(('ctx', 'fsdp')), may hold values from -0.3125 to 0.3125
- w_out: bfloat16 [1024, 1024], P(('ctx', 'fsdp')), may hold values from -1.5 to 1.5
- b_out: bfloat16 [1024], P(('ctx', 'fsdp')), may hold values from -1.75 to 1.75
- ln1_gain: bfloat16 [1024], P(('ctx', 'fsdp')), may hold values from 0.5 to 1.5
- ln1_bias: bfloat16 [1024], P(('ctx', 'fsdp')), may hold values from -1.75 to 1.75
- w_up: bfloat16 [1024, 4096], P(('ctx', 'fsdp')), may hold values from -0.1875 to 0.1875
- b_up: bfloat16 [4096], P(('ctx', 'fsdp')), may hold values from -1.75 to 1.75
- w_down: bfloat16 [4096, 1024], P(('ctx', 'fsdp')), may hold values from -0.09375 to 0.09375
- b_down: bfloat16 [1024], P(('ctx', 'fsdp')), may hold values from -1.75 to 1.75
- ln2_gain: bfloat16 [1024], P(('ctx', 'fsdp')), may hold values from 0.5 to 1.5
- ln2_bias: bfloat16 [1024], P(('ctx', 'fsdp')), may hold values from -1.75 to 1.75
- cotangent: bfloat16 [2, 8, 1024, 1024], P(None, 'fsdp', 'ctx'), may hold values from -6 to 6
Outputs:
- output: bfloat16 [2, 8, 1024, 1024], P(None, 'fsdp', 'ctx')
- grad_tokens: float32 [2, 8, 1024, 1024], P(None, 'fsdp', 'ctx')
- grad_w_query: float32 [1024, 1024], P(('ctx', 'fsdp'))
- grad_b_query: float32 [1024], P(('ctx', 'fsdp'))
- grad_w_key: float32 [1024, 1024], P(('ctx', 'fsdp'))
- grad_w_value: float32 [1024, 1024], P(('ctx', 'fsdp'))
- grad_b_value: float32 [1024], P(('ctx', 'fsdp'))
- grad_w_out: float32 [1024, 1024], P(('ctx', 'fsdp'))
- grad_b_out: float32 [1024], P(('ctx', 'fsdp'))
- grad_ln1_gain: float32 [1024], P(('ctx', 'fsdp'))
- grad_ln1_bias: float32 [1024], P(('ctx', 'fsdp'))
- grad_w_up: float32 [1024, 4096], P(('ctx', 'fsdp'))
- grad_b_up: float32 [4096], P(('ctx', 'fsdp'))
- grad_w_down: float32 [4096, 1024], P(('ctx', 'fsdp'))
- grad_b_down: float32 [1024], P(('ctx', 'fsdp'))
- grad_ln2_gain: float32 [1024], P(('ctx', 'fsdp'))
- grad_ln2_bias: float32 [1024], P(('ctx', 'fsdp'))
Inputs may be any that keep to these rules, and one draw needn't show every extreme that they name: `doc_lengths`: in each stream the 4 documents fill the 1024 positions in order, and the longest is exactly 512.
All inputs are finite; a program needn't handle non-finite values.
Results may differ from a plain program's by a relative error of at most 0.014.
Values may be sent and summed in bfloat16 or wider, within the bound.
No kernel may reach another device: no remote copies, remote signals or barrier semaphores. Data moves between devices by JAX's collectives and lax.ppermute only.
A program may use at most 256 MiB of HBM per device.

v0:
```python
import jax
import jax.numpy as jnp
from jax import lax
from jax.sharding import PartitionSpec as P

H = 16
HD = 64
EPSILON = 1e-12
SCORE_SCALE = 0.125
MASKED_SCORE = -1e30


def exact_gelu(values_in):
    return jax.nn.gelu(values_in, approximate=False)


def norm_forward(values_in, gain_vec, bias_vec):
    center = values_in - jnp.mean(values_in, axis=-1, keepdims=True)
    inverse = lax.rsqrt(jnp.mean(center * center, axis=-1, keepdims=True) + EPSILON)
    normed = center * inverse
    return (normed * gain_vec + bias_vec, normed, inverse)


def norm_backward(upstream, normed, inverse, gain_vec):
    scaled = upstream * gain_vec
    inner_sum = (
        scaled
        - jnp.mean(scaled, axis=-1, keepdims=True)
        - normed * jnp.mean(scaled * normed, axis=-1, keepdims=True)
    )
    return (inverse * inner_sum, jnp.sum(upstream * normed, axis=0), jnp.sum(upstream, axis=0))


def segment_ids(lengths, positions):
    starts = jnp.cumsum(lengths) - lengths
    return jnp.sum((positions[:, None] >= starts[None, :]).astype(jnp.int32), axis=1) - 1


def to_blocks(stacked):
    streams, row_count, _ = stacked.shape
    pieces = stacked.reshape(streams, row_count, H // 4, 4, HD)
    return jnp.moveaxis(pieces, 2, 1).reshape(streams * (H // 4), row_count, 4, HD)


def from_blocks(stacked, streams):
    _, row_count, heads_block, head_size = stacked.shape
    pieces = stacked.reshape(streams, H // 4, row_count, heads_block, head_size)
    return jnp.moveaxis(pieces, 1, 2).reshape(streams, row_count, H * HD)


def masked_scores(queries, keys_all, seg_rows, seg_cols):
    scores = (
        jnp.einsum("qgd,kgd->gqk", queries, keys_all, preferred_element_type=jnp.float32)
        * SCORE_SCALE
    )
    return jnp.where((seg_rows[:, None] == seg_cols[None, :])[None], scores, MASKED_SCORE)


def attend(operands):
    queries, keys_all, values_all, seg_rows, seg_cols = operands
    scores = masked_scores(queries, keys_all, seg_rows, seg_cols)
    top_score = jnp.max(scores, axis=-1, keepdims=True)
    exponent_terms = jnp.exp(scores - top_score)
    totals = jnp.sum(exponent_terms, axis=-1, keepdims=True)
    probs = exponent_terms / totals
    mixed = jnp.einsum(
        "gqk,kgd->qgd", probs.astype(jnp.bfloat16), values_all, preferred_element_type=jnp.float32
    )
    return (mixed, top_score + jnp.log(totals))


def attend_back(operands):
    queries, keys_all, values_all, seg_rows, seg_cols, log_totals, grad_mixed = operands
    scores = masked_scores(queries, keys_all, seg_rows, seg_cols)
    probs = jnp.exp(scores - log_totals)
    grad_values = jnp.einsum(
        "gqk,qgd->kgd", probs.astype(jnp.bfloat16), grad_mixed, preferred_element_type=jnp.float32
    )
    grad_probs = jnp.einsum(
        "qgd,kgd->gqk", grad_mixed, values_all, preferred_element_type=jnp.float32
    )
    central = jnp.sum(probs * grad_probs, axis=-1, keepdims=True)
    grad_scores = (probs * (grad_probs - central)).astype(jnp.bfloat16)
    grad_queries = (
        jnp.einsum("gqk,kgd->qgd", grad_scores, keys_all, preferred_element_type=jnp.float32)
        * SCORE_SCALE
    )
    grad_keys = (
        jnp.einsum("gqk,qgd->kgd", grad_scores, queries, preferred_element_type=jnp.float32)
        * SCORE_SCALE
    )
    return (grad_queries, grad_keys, grad_values)


def left_product(left, right):
    return jnp.einsum("ta,tb->ab", left, right, preferred_element_type=jnp.float32)


def right_transpose(left, right):
    return jnp.einsum("tb,ab->ta", left, right, preferred_element_type=jnp.float32)


def body(
    tokens,
    doc_lengths,
    w_query,
    b_query,
    w_key,
    w_value,
    b_value,
    w_out,
    b_out,
    ln1_gain,
    ln1_bias,
    w_up,
    b_up,
    w_down,
    b_down,
    ln2_gain,
    ln2_bias,
    cotangent,
):
    micro, per_device, ctx_rows, width = tokens.shape
    stream_len = ctx_rows * lax.axis_size("ctx")
    row_pos = lax.axis_index("ctx") * ctx_rows + jnp.arange(ctx_rows, dtype=jnp.int32)
    key_pos = jnp.arange(stream_len, dtype=jnp.int32)
    blocks_per = H // 4
    flat_rows = per_device * ctx_rows
    outputs = []
    input_grads = []
    accumulated = None
    for batch_index in range(micro):
        full = (
            lax.all_gather(w_query, ("ctx", "fsdp"), axis=0, tiled=True),
            lax.all_gather(b_query, ("ctx", "fsdp"), axis=0, tiled=True),
            lax.all_gather(w_key, ("ctx", "fsdp"), axis=0, tiled=True),
            lax.all_gather(w_value, ("ctx", "fsdp"), axis=0, tiled=True),
            lax.all_gather(b_value, ("ctx", "fsdp"), axis=0, tiled=True),
            lax.all_gather(w_out, ("ctx", "fsdp"), axis=0, tiled=True),
            lax.all_gather(b_out, ("ctx", "fsdp"), axis=0, tiled=True),
            lax.all_gather(ln1_gain, ("ctx", "fsdp"), axis=0, tiled=True),
            lax.all_gather(ln1_bias, ("ctx", "fsdp"), axis=0, tiled=True),
            lax.all_gather(w_up, ("ctx", "fsdp"), axis=0, tiled=True),
            lax.all_gather(b_up, ("ctx", "fsdp"), axis=0, tiled=True),
            lax.all_gather(w_down, ("ctx", "fsdp"), axis=0, tiled=True),
            lax.all_gather(b_down, ("ctx", "fsdp"), axis=0, tiled=True),
            lax.all_gather(ln2_gain, ("ctx", "fsdp"), axis=0, tiled=True),
            lax.all_gather(ln2_bias, ("ctx", "fsdp"), axis=0, tiled=True),
        )
        (
            query_mat,
            query_bias,
            key_mat,
            value_mat,
            value_bias,
            out_mat,
            out_bias,
            gain_one,
            bias_one,
            up_mat,
            up_bias,
            down_mat,
            down_bias,
            gain_two,
            bias_two,
        ) = full
        inputs = tokens[batch_index].reshape(flat_rows, width)
        queries = (
            jnp.dot(inputs, query_mat, preferred_element_type=jnp.float32) + query_bias
        ).astype(jnp.bfloat16)
        keys_mine = jnp.dot(inputs, key_mat, preferred_element_type=jnp.float32).astype(
            jnp.bfloat16
        )
        values_mine = (
            jnp.dot(inputs, value_mat, preferred_element_type=jnp.float32) + value_bias
        ).astype(jnp.bfloat16)
        keys_all, values_all = (
            lax.all_gather(
                keys_mine.reshape(per_device, ctx_rows, width), "ctx", axis=1, tiled=True
            ),
            lax.all_gather(
                values_mine.reshape(per_device, ctx_rows, width), "ctx", axis=1, tiled=True
            ),
        )
        lengths_now = doc_lengths[batch_index]
        seg_rows = jax.vmap(segment_ids, (0, None))(lengths_now, row_pos)
        seg_cols = jax.vmap(segment_ids, (0, None))(lengths_now, key_pos)
        rows_rep = jnp.repeat(seg_rows, blocks_per, axis=0)
        cols_rep = jnp.repeat(seg_cols, blocks_per, axis=0)
        query_blocks = to_blocks(queries.reshape(per_device, ctx_rows, width))
        key_blocks = to_blocks(keys_all)
        value_blocks = to_blocks(values_all)
        mixed_blocks, log_totals = lax.map(
            attend, (query_blocks, key_blocks, value_blocks, rows_rep, cols_rep)
        )
        mixed = from_blocks(mixed_blocks, per_device).reshape(flat_rows, width).astype(jnp.bfloat16)
        attended = jnp.dot(mixed, out_mat, preferred_element_type=jnp.float32) + out_bias
        first, normed_one, inverse_one = norm_forward(
            inputs.astype(jnp.float32) + attended, gain_one, bias_one
        )
        first_low = first.astype(jnp.bfloat16)
        hidden = jnp.dot(first_low, up_mat, preferred_element_type=jnp.float32) + up_bias
        activated_full, gelu_pull = jax.vjp(exact_gelu, hidden)
        activated = activated_full.astype(jnp.bfloat16)
        branch = jnp.dot(activated, down_mat, preferred_element_type=jnp.float32) + down_bias
        result, normed_two, inverse_two = norm_forward(first + branch, gain_two, bias_two)
        outputs.append(result.astype(jnp.bfloat16).reshape(per_device, ctx_rows, width))
        full = (
            lax.all_gather(w_query, ("ctx", "fsdp"), axis=0, tiled=True),
            lax.all_gather(b_query, ("ctx", "fsdp"), axis=0, tiled=True),
            lax.all_gather(w_key, ("ctx", "fsdp"), axis=0, tiled=True),
            lax.all_gather(w_value, ("ctx", "fsdp"), axis=0, tiled=True),
            lax.all_gather(b_value, ("ctx", "fsdp"), axis=0, tiled=True),
            lax.all_gather(w_out, ("ctx", "fsdp"), axis=0, tiled=True),
            lax.all_gather(b_out, ("ctx", "fsdp"), axis=0, tiled=True),
            lax.all_gather(ln1_gain, ("ctx", "fsdp"), axis=0, tiled=True),
            lax.all_gather(ln1_bias, ("ctx", "fsdp"), axis=0, tiled=True),
            lax.all_gather(w_up, ("ctx", "fsdp"), axis=0, tiled=True),
            lax.all_gather(b_up, ("ctx", "fsdp"), axis=0, tiled=True),
            lax.all_gather(w_down, ("ctx", "fsdp"), axis=0, tiled=True),
            lax.all_gather(b_down, ("ctx", "fsdp"), axis=0, tiled=True),
            lax.all_gather(ln2_gain, ("ctx", "fsdp"), axis=0, tiled=True),
            lax.all_gather(ln2_bias, ("ctx", "fsdp"), axis=0, tiled=True),
        )
        (
            query_mat,
            query_bias,
            key_mat,
            value_mat,
            value_bias,
            out_mat,
            out_bias,
            gain_one,
            bias_one,
            up_mat,
            up_bias,
            down_mat,
            down_bias,
            gain_two,
            bias_two,
        ) = full
        upstream = cotangent[batch_index].reshape(flat_rows, width).astype(jnp.float32)
        grad_h2, grad_gain_two, grad_bias_two = norm_backward(
            upstream, normed_two, inverse_two, gain_two
        )
        grad_branch = grad_h2.astype(jnp.bfloat16)
        grad_down_bias = jnp.sum(grad_branch.astype(jnp.float32), axis=0)
        grad_down_mat = left_product(activated, grad_branch)
        grad_activated = right_transpose(grad_branch, down_mat)
        grad_hidden = gelu_pull(grad_activated)[0].astype(jnp.bfloat16)
        grad_up_bias = jnp.sum(grad_hidden.astype(jnp.float32), axis=0)
        grad_up_mat = left_product(first_low, grad_hidden)
        grad_first = right_transpose(grad_hidden, up_mat) + grad_h2
        grad_h1, grad_gain_one, grad_bias_one = norm_backward(
            grad_first, normed_one, inverse_one, gain_one
        )
        grad_attended = grad_h1.astype(jnp.bfloat16)
        grad_out_bias = jnp.sum(grad_attended.astype(jnp.float32), axis=0)
        grad_out_mat = left_product(mixed, grad_attended)
        grad_mixed = right_transpose(grad_attended, out_mat).astype(jnp.bfloat16)
        grad_mixed_blocks = to_blocks(grad_mixed.reshape(per_device, ctx_rows, width))
        grad_query_blocks, grad_key_blocks, grad_value_blocks = lax.map(
            attend_back,
            (
                query_blocks,
                key_blocks,
                value_blocks,
                rows_rep,
                cols_rep,
                log_totals,
                grad_mixed_blocks,
            ),
        )
        grad_keys_all = from_blocks(grad_key_blocks, per_device)
        grad_values_all = from_blocks(grad_value_blocks, per_device)
        grad_keys_mine, grad_values_mine = (
            lax.psum_scatter(
                grad_keys_all.astype(jnp.bfloat16), "ctx", scatter_dimension=1, tiled=True
            ).astype(jnp.float32),
            lax.psum_scatter(
                grad_values_all.astype(jnp.bfloat16), "ctx", scatter_dimension=1, tiled=True
            ).astype(jnp.float32),
        )
        grad_queries = (
            from_blocks(grad_query_blocks, per_device)
            .reshape(flat_rows, width)
            .astype(jnp.bfloat16)
        )
        grad_keys = grad_keys_mine.reshape(flat_rows, width).astype(jnp.bfloat16)
        grad_values = grad_values_mine.reshape(flat_rows, width).astype(jnp.bfloat16)
        grad_query_bias = jnp.sum(grad_queries.astype(jnp.float32), axis=0)
        grad_value_bias = jnp.sum(grad_values.astype(jnp.float32), axis=0)
        grad_query_mat = left_product(inputs, grad_queries)
        grad_key_mat = left_product(inputs, grad_keys)
        grad_value_mat = left_product(inputs, grad_values)
        grad_inputs = (
            grad_h1
            + right_transpose(grad_queries, query_mat)
            + right_transpose(grad_keys, key_mat)
            + right_transpose(grad_values, value_mat)
        )
        input_grads.append(grad_inputs.reshape(per_device, ctx_rows, width))
        owned = (
            lax.psum_scatter(grad_query_mat, ("ctx", "fsdp"), scatter_dimension=0, tiled=True),
            lax.psum_scatter(grad_query_bias, ("ctx", "fsdp"), scatter_dimension=0, tiled=True),
            lax.psum_scatter(grad_key_mat, ("ctx", "fsdp"), scatter_dimension=0, tiled=True),
            lax.psum_scatter(grad_value_mat, ("ctx", "fsdp"), scatter_dimension=0, tiled=True),
            lax.psum_scatter(grad_value_bias, ("ctx", "fsdp"), scatter_dimension=0, tiled=True),
            lax.psum_scatter(grad_out_mat, ("ctx", "fsdp"), scatter_dimension=0, tiled=True),
            lax.psum_scatter(grad_out_bias, ("ctx", "fsdp"), scatter_dimension=0, tiled=True),
            lax.psum_scatter(grad_gain_one, ("ctx", "fsdp"), scatter_dimension=0, tiled=True),
            lax.psum_scatter(grad_bias_one, ("ctx", "fsdp"), scatter_dimension=0, tiled=True),
            lax.psum_scatter(grad_up_mat, ("ctx", "fsdp"), scatter_dimension=0, tiled=True),
            lax.psum_scatter(grad_up_bias, ("ctx", "fsdp"), scatter_dimension=0, tiled=True),
            lax.psum_scatter(grad_down_mat, ("ctx", "fsdp"), scatter_dimension=0, tiled=True),
            lax.psum_scatter(grad_down_bias, ("ctx", "fsdp"), scatter_dimension=0, tiled=True),
            lax.psum_scatter(grad_gain_two, ("ctx", "fsdp"), scatter_dimension=0, tiled=True),
            lax.psum_scatter(grad_bias_two, ("ctx", "fsdp"), scatter_dimension=0, tiled=True),
        )
        accumulated = owned if accumulated is None else jax.tree.map(jnp.add, accumulated, owned)
    stacked_out = jnp.stack(outputs)
    stacked_grads = jnp.stack(input_grads)
    return (
        stacked_out,
        stacked_grads,
        accumulated[0],
        accumulated[1],
        accumulated[2],
        accumulated[3],
        accumulated[4],
        accumulated[5],
        accumulated[6],
        accumulated[7],
        accumulated[8],
        accumulated[9],
        accumulated[10],
        accumulated[11],
        accumulated[12],
        accumulated[13],
        accumulated[14],
    )


def solution(mesh):
    placed = (
        P(None, "fsdp", "ctx", None),
        P(None, "fsdp", None),
        P(("ctx", "fsdp"), None),
        P(("ctx", "fsdp")),
        P(("ctx", "fsdp"), None),
        P(("ctx", "fsdp"), None),
        P(("ctx", "fsdp")),
        P(("ctx", "fsdp"), None),
        P(("ctx", "fsdp")),
        P(("ctx", "fsdp")),
        P(("ctx", "fsdp")),
        P(("ctx", "fsdp"), None),
        P(("ctx", "fsdp")),
        P(("ctx", "fsdp"), None),
        P(("ctx", "fsdp")),
        P(("ctx", "fsdp")),
        P(("ctx", "fsdp")),
        P(None, "fsdp", "ctx", None),
    )
    return jax.shard_map(
        body,
        mesh=mesh,
        in_specs=placed,
        out_specs=(
            P(None, "fsdp", "ctx", None),
            P(None, "fsdp", "ctx", None),
            P(("ctx", "fsdp"), None),
            P(("ctx", "fsdp")),
            P(("ctx", "fsdp"), None),
            P(("ctx", "fsdp"), None),
            P(("ctx", "fsdp")),
            P(("ctx", "fsdp"), None),
            P(("ctx", "fsdp")),
            P(("ctx", "fsdp")),
            P(("ctx", "fsdp")),
            P(("ctx", "fsdp"), None),
            P(("ctx", "fsdp")),
            P(("ctx", "fsdp"), None),
            P(("ctx", "fsdp")),
            P(("ctx", "fsdp")),
            P(("ctx", "fsdp")),
        ),
        check_vma=False,
    )
```

profile of v0, /device:TPU:0, one launch (start us, length us, event | category | flops | bytes accessed | tf_op | source)
XLA Modules:
  0.0 1791.1 jit_solution(13232261122871129861)
XLA Ops:
  16.2 42.3 %all-reduce.18 = (bf16[1024]{0:T(1024)(128)(2,1)S(1)}, bf16[1024]{0:T(1024)(128)(2,1)S(1)}, bf16[1024]{0:T(1024)(128)(2,1)S(1)}, bf16[1024]{0:T(1024)(128)(2,1)S...) all-reduce(bf16[1024]{0:T(1024)(128)(2,1)S(1)} %dynamic-update-slic, ...), channel_id=1, replica_groups=mesh['ctx'=4,'fsdp'=8] {'ctx','fsdp'}, use_global_device_ids=true, to_apply=%add | all-reduce | flops 8192 | bytes 32768
  58.5 11.8 all-gather.16.cloned.1.call-done
  70.2 3.4 fusion.134
  73.7 55.0 %all-gather.20.cloned.1.call-done = bf16[1024,1024]{1,0:T(8,128)(2,1)} async-done(((bf16[32,1024]{1,0:T(8,128)(2,1)}), bf16[1024,1024]{1,0:T(8,128)(2,1)}) %all-gather.20.cloned.1.call-update) | async-done | bytes 2097168 | tf_op jit(solution)/shard_map/all_gather | solution.py:136
  128.8 3.1 convolution_convert_fusion.3
  133.5 3.1 convolution_convert_fusion.2
  138.8 39.2 %all-gather.4 = bf16[32,1,128]{2,1,0:T(2,128)(2,1)S(1)} all-gather(bf16[1,1,128]{2,1,0:T(2,128)(2,1)S(1)} %bitcast.493), channel_id=1, replica_groups=mesh['ctx'=4,'fsdp'=8] {'ctx','fsdp'}, dimensions={0}, use_global_device_ids=true | all-gather | bytes 8448 | tf_op jit(solution)/shard_map/all_gather | solution.py:144
  179.9 7.2 all-gather.18.cloned.1.call-done
  187.1 3.2 fusion.135
  196.0 27.7 %all-gather.28.cloned.1.call-done = bf16[1024,1024]{1,0:T(8,128)(2,1)} async-done(((bf16[256,1024]{1,0:T(8,128)(2,1)}), bf16[1024,1024]{1,0:T(8,128)(2,1)}) %all-gather.28.cloned.1.call-update) | async-done | bytes 2097168 | tf_op jit(solution)/shard_map/all_gather | solution.py:181
  223.7 4.4 copy.68
  228.0 33.2 %all-gather.30.cloned.1.call-done = bf16[1024,1024]{1,0:T(8,128)(2,1)} async-done(((bf16[256,1024]{1,0:T(8,128)(2,1)}), bf16[1024,1024]{1,0:T(8,128)(2,1)}) %all-gather.30.cloned.1.call-update) | async-done | bytes 2097168 | tf_op jit(solution)/shard_map/all_gather | solution.py:178
  261.3 2.9 copy.70
  265.0 26.7 %while.52 = (s32[]{:T(128)}, bf16[4,256,4,64]{1,3,2,0:T(8,128)(2,1)}, f32[4,4,256,1]{2,1,3,0:T(4,128)S(1)}, bf16[4,1024,4,64]{1,3,2,0:T(8,128)(2,1)}, s32[4,256]...) while((s32[]{:T(128)}, ...), condition=%wide.region_6.7_spmd, body=%wide.region_3.6_spmd.sunk | while | flops 281279488 | bytes 19317928 | solution.py:193
  291.7 6.6 all-gather.32.cloned.1.call-done
  298.3 3.9 copy.71
  302.2 33.2 %all-gather.34.cloned.1.call-done = bf16[1024,1024]{1,0:T(8,128)(2,1)} async-done(((bf16[256,1024]{1,0:T(8,128)(2,1)}), bf16[1024,1024]{1,0:T(8,128)(2,1)}) %all-gather.34.cloned.1.call-update) | async-done | bytes 2097168 | tf_op jit(solution)/shard_map/all_gather | solution.py:178
  335.5 2.9 copy.73
  338.4 56.6 %all-gather.22.cloned.1.call-done = bf16[1024,1024]{1,0:T(8,128)(2,1)} async-done(((bf16[32,1024]{1,0:T(8,128)(2,1)}), bf16[1024,1024]{1,0:T(8,128)(2,1)}) %all-gather.22.cloned.1.call-update) | async-done | bytes 2097168 | tf_op jit(solution)/shard_map/all_gather | solution.py:139
  398.9 23.4 %while.53 = (s32[]{:T(128)}, bf16[4,256,4,64]{1,3,2,0:T(8,128)(2,1)S(1)}, f32[4,4,256,1]{2,1,3,0:T(4,128)S(1)}, bf16[4,1024,4,64]{1,3,2,0:T(8,128)(2,1)}, s32[4,...) while((s32[]{:T(128)}, ...), condition=%wide.region_17.18_spmd, body=%wide.region_14.17_spmd.sunk | while | flops 281279488 | bytes 15123569 | solution.py:193
  423.1 3.0 fusion.213
  426.4 47.9 %all-gather.24.cloned.1.call-done = bf16[1024,4096]{1,0:T(8,128)(2,1)} async-done(((bf16[32,4096]{1,0:T(8,128)(2,1)}), bf16[1024,4096]{1,0:T(8,128)(2,1)}) %all-gather.24.cloned.1.call-update) | async-done | bytes 8388624 | tf_op jit(solution)/shard_map/all_gather | solution.py:143
  474.3 16.4 multiply_convert_fusion.3
  490.7 62.5 %all-gather.26.cloned.1.call-done = bf16[4096,1024]{1,0:T(8,128)(2,1)} async-done(((bf16[128,1024]{1,0:T(8,128)(2,1)}), bf16[4096,1024]{1,0:T(8,128)(2,1)}) %all-gather.26.cloned.1.call-update) | async-done | bytes 8388624 | tf_op jit(solution)/shard_map/all_gather | solution.py:145
  553.2 6.8 fusion.212
  560.3 13.4 multiply_convert_fusion.2
  580.6 13.1 convert_reduce_fusion.1
  593.7 7.4 multiply_reduce_fusion.3
  601.2 11.9 convert_reduce_fusion
  613.0 8.6 convert_reduce_fusion.7
  625.4 2.8 convolution_convert_fusion.1
  632.5 45.7 %while.54 = (s32[]{:T(128)}, bf16[4,256,4,64]{1,3,2,0:T(8,128)(2,1)S(1)}, bf16[4,1024,4,64]{1,3,2,0:T(8,128)(2,1)}, bf16[4,1024,4,64]{1,3,2,0:T(8,128)(2,1)}, bf...) while((s32[]{:T(128)}, ...), condition=%wide.region_28.29_spmd, body=%wide.region_26.28_spmd.sunk | while | flops 687406080 | bytes 72663312 | solution.py:262
  635.6 2.8 multiply_reduce_fusion.14
  647.0 2.8 multiply_reduce_fusion.14
  658.4 2.8 multiply_reduce_fusion.14
  669.8 2.8 multiply_reduce_fusion.14
  682.3 45.9 %while.55 = (s32[]{:T(128)}, bf16[4,256,4,64]{1,3,2,0:T(8,128)(2,1)}, bf16[4,1024,4,64]{1,3,2,0:T(8,128)(2,1)}, bf16[4,1024,4,64]{1,3,2,0:T(8,128)(2,1)}, bf16[4...) while((s32[]{:T(128)}, ...), condition=%wide.region_37.38_spmd, body=%wide.region_35.37_spmd.sunk | while | flops 687406080 | bytes 76857680 | solution.py:262
  685.5 2.8 multiply_reduce_fusion.15
  697.0 2.8 multiply_reduce_fusion.15
  708.4 2.8 multiply_reduce_fusion.15
  719.8 2.8 multiply_reduce_fusion.15
  733.4 5.4 copy.79
  744.0 3.7 fusion.157
  747.7 14.6 reduce-scatter.21.cloned.1.call-done
  762.3 5.0 add_bitcast_fusion.1
  767.3 5.3 copy.81
  772.7 27.8 %reduce-scatter.19.cloned.1.call-done = bf16[1,256,1024]{1,2,0:T(8,128)(2,1)} async-done(((bf16[1,1024,1024]{1,2,0:T(8,128)(2,1)}), bf16[1,256,1024]{1,2,0:T(8,128)(2,1)}) %reduce-scatter.19.cloned.1.call-update) | async-done | bytes 524304 | tf_op jit(solution)/shard_map/reduce_scatter | solution.py:280
  800.5 3.7 fusion.154
  804.2 34.6 %reduce-scatter.23.cloned.1.call-done = bf16[1,256,1024]{1,2,0:T(8,128)(2,1)} async-done(((bf16[1,1024,1024]{1,2,0:T(8,128)(2,1)}), bf16[1,256,1024]{1,2,0:T(8,128)(2,1)}) %reduce-scatter.23.cloned.1.call-update) | async-done | bytes 524304 | tf_op jit(solution)/shard_map/reduce_scatter | solution.py:280
  838.8 5.0 add_bitcast_fusion
  843.8 5.4 copy.83
  849.9 4.4 fusion.203
  854.3 10.0 convolution_add_fusion.1
  865.5 4.0 fusion.195
  869.5 10.1 convolution_add_fusion
  886.9 3.4 convolution_add_fusion.7
  892.6 40.6 %all-reduce.17 = (f32[1024]{0:T(1024)S(1)}, f32[1024]{0:T(1024)S(1)}, f32[1024]{0:T(1024)S(1)}, f32[1024]{0:T(1024)S(1)}, f32[1024]{0:T(1024)S(1)}, /*index=5*/f...) all-reduce(f32[1024]{0:T(1024)S(1)} %reshape.711, ...), channel_id=26, replica_groups=mesh['ctx'=4,'fsdp'=8] {'ctx','fsdp'}, use_global_device_ids=true, to_apply=%region_43.44.clone | all-reduce | flops 12288 | bytes 98304
  938.5 2.9 convolution_add_fusion.6
  945.3 39.1 %reduce-scatter.31.cloned.1.call-done = f32[32,1024]{1,0:T(8,128)} async-done(((f32[1024,1024]{1,0:T(8,128)}), f32[32,1024]{1,0:T(8,128)}) %reduce-scatter.31.cloned.1.call-update) | async-done | bytes 131088
  984.3 142.3 %reduce-scatter.25.cloned.1.call-done = f32[32,1024]{1,0:T(8,128)} async-done(((f32[1024,1024]{1,0:T(8,128)}), f32[32,1024]{1,0:T(8,128)}) %reduce-scatter.25.cloned.1.call-update) | async-done | bytes 131088 | tf_op jit(solution)/shard_map/reduce_scatter | solution.py:309
  1126.6 141.8 %reduce-scatter.33.cloned.1.call-done = f32[32,1024]{1,0:T(8,128)} async-done(((f32[1024,1024]{1,0:T(8,128)}), f32[32,1024]{1,0:T(8,128)}) %reduce-scatter.33.cloned.1.call-update) | async-done | bytes 131088
  1268.4 142.2 %reduce-scatter.35.cloned.1.call-done = f32[32,1024]{1,0:T(8,128)} async-done(((f32[1024,1024]{1,0:T(8,128)}), f32[32,1024]{1,0:T(8,128)}) %reduce-scatter.35.cloned.1.call-update) | async-done | bytes 131088
  1410.6 186.4 %reduce-scatter.27.cloned.1.call-done = f32[32,4096]{1,0:T(8,128)} async-done(((f32[1024,4096]{1,0:T(8,128)}), f32[32,4096]{1,0:T(8,128)}) %reduce-scatter.27.cloned.1.call-update) | async-done | bytes 524304 | tf_op jit(solution)/shard_map/reduce_scatter | solution.py:313
  1597.0 187.1 %reduce-scatter.29.cloned.1.call-done = f32[128,1024]{1,0:T(8,128)} async-done(((f32[4096,1024]{1,0:T(8,128)}), f32[128,1024]{1,0:T(8,128)}) %reduce-scatter.29.cloned.1.call-update) | async-done | bytes 524304 | tf_op jit(solution)/shard_map/reduce_scatter | solution.py:315
  (548 shorter events, 193.7 us)
Async XLA Ops:
  7.2 121.6 %copy-start.7 = (bf16[2,1,256,1024]{3,2,1,0:T(8,128)(2,1)S(1)}, bf16[2,1,256,1024]{3,2,1,0:T(8,128)(2,1)}, u32[]{:S(2)}) copy-start(bf16[2,1,256,1024]{3,2,1,0:T(8,128)(2,1)} %param.26) | copy-start | bytes 3145732
  7.2 63.0 %all-gather.16.cloned.1.call-start = ((), (), s32[]{:S(2)}) async-start(), calls=%async_computation.10 | async-start | bytes 2162688 | tf_op jit(solution)/shard_map/all_gather | solution.py:137
  7.9 120.8 %all-gather.20.cloned.1.call-start = ((), (), s32[]{:S(2)}) async-start(), calls=%async_computation.12 | async-start | bytes 2162688 | tf_op jit(solution)/shard_map/all_gather | solution.py:136
  8.7 178.4 %all-gather.18.cloned.1.call-start = ((), (), s32[]{:S(2)}) async-start(), calls=%async_computation.11 | async-start | bytes 2162688 | tf_op jit(solution)/shard_map/all_gather | solution.py:134
  9.4 214.2 %all-gather.28.cloned.1.call-start = ((), (), s32[]{:S(2)}) async-start(), calls=%async_computation.20 | async-start | bytes 2621440 | tf_op jit(solution)/shard_map/all_gather | solution.py:181
  70.2 61.7 %copy-start.22 = (bf16[1024,1024]{1,0:T(8,128)(2,1)S(1)}, bf16[1024,1024]{1,0:T(8,128)(2,1)}, u32[]{:S(2)}) copy-start(bf16[1024,1024]{1,0:T(8,128)(2,1)} %all-gather.16.cloned.1.call-done) | copy-start | bytes 6291460
  73.7 187.6 %all-gather.30.cloned.1.call-start = ((), (), s32[]{:S(2)}) async-start(), calls=%async_computation.21 | async-start | bytes 2621440 | tf_op jit(solution)/shard_map/all_gather | solution.py:178
  131.9 6.9 copy-start.85
  131.9 46.2 %copy-start.84 = (s32[2,1,4]{2,1,0:T(1,128)S(1)}, s32[2,1,4]{2,1,0:T(1,128)}, u32[]{:S(2)}) copy-start(s32[2,1,4]{2,1,0:T(1,128)} %param.27) | copy-start | bytes 100
  131.9 166.4 %all-gather.32.cloned.1.call-start = ((), (), s32[]{:S(2)}) async-start(), calls=%async_computation.22 | async-start | bytes 2621440 | tf_op jit(solution)/shard_map/all_gather | solution.py:181
  133.5 202.0 %all-gather.34.cloned.1.call-start = ((), (), s32[]{:S(2)}) async-start(), calls=%async_computation.23 | async-start | bytes 2621440 | tf_op jit(solution)/shard_map/all_gather | solution.py:178
  136.6 258.3 %all-gather.22.cloned.1.call-start = ((), (), s32[]{:S(2)}) async-start(), calls=%async_computation.13 | async-start | bytes 2162688 | tf_op jit(solution)/shard_map/all_gather | solution.py:139
  137.4 336.9 %all-gather.24.cloned.1.call-start = ((), (), s32[]{:S(2)}) async-start(), calls=%async_computation.14 | async-start | bytes 8650752 | tf_op jit(solution)/shard_map/all_gather | solution.py:143
  138.1 415.1 %all-gather.26.cloned.1.call-start = ((), (), s32[]{:S(2)}) async-start(), calls=%async_computation.15 | async-start | bytes 8650752 | tf_op jit(solution)/shard_map/all_gather | solution.py:145
  138.7 605.3 %reduce-scatter.17.cloned.1.call-start = ((), (), s32[]{:S(2)}) async-start(), calls=%async_computation.16 | async-start | bytes 2621440 | tf_op jit(solution)/shard_map/reduce_scatter | solution.py:277
  178.7 395.0 %copy-start.53 = (f32[1024]{0:T(1024)}, f32[1024]{0:T(1024)S(1)}, u32[]{:S(2)}) copy-start(f32[1024]{0:T(1024)S(1)} %convert_element_type.386) | copy-start | bytes 12292
  187.1 5.3 copy-start.25
  291.7 10.5 copy-start.2
  291.7 46.6 %copy-start.56 = (s32[4,1024]{1,0:T(4,128)}, s32[4,1024]{1,0:T(4,128)S(1)}, u32[]{:S(2)}) copy-start(s32[4,1024]{1,0:T(4,128)S(1)} %get-tuple-element.908) | copy-start | bytes 49156
  291.7 46.7 %copy-start.57 = (f32[4,4,256,1]{2,1,3,0:T(4,128)}, f32[4,4,256,1]{2,1,3,0:T(4,128)S(1)}, u32[]{:S(2)}) copy-start(f32[4,4,256,1]{2,1,3,0:T(4,128)S(1)} %get-tuple-element.809) | copy-start | bytes 49156
  291.7 46.7 %copy-start.60 = (s32[4,256]{1,0:T(4,128)}, s32[4,256]{1,0:T(4,128)S(1)}, u32[]{:S(2)}) copy-start(s32[4,256]{1,0:T(4,128)S(1)} %get-tuple-element.918) | copy-start | bytes 12292
  422.3 68.4 %copy-start = (bf16[4,1024,4,64]{1,3,2,0:T(8,128)(2,1)}, bf16[4,1024,4,64]{1,3,2,0:T(8,128)(2,1)S(1)}, u32[]{:S(2)}) copy-start(bf16[4,1024,4,64]{1,3,2,0:T(8,128)(2,1)S(1)} %get-tuple-element.861) | copy-start | bytes 6291460
  422.3 68.4 %copy-start.55 = (s32[4,1024]{1,0:T(4,128)}, s32[4,1024]{1,0:T(4,128)S(1)}, u32[]{:S(2)}) copy-start(s32[4,1024]{1,0:T(4,128)S(1)} %get-tuple-element.907) | copy-start | bytes 49156
  422.3 68.4 %copy-start.58 = (f32[4,4,256,1]{2,1,3,0:T(4,128)}, f32[4,4,256,1]{2,1,3,0:T(4,128)S(1)}, u32[]{:S(2)}) copy-start(f32[4,4,256,1]{2,1,3,0:T(4,128)S(1)} %get-tuple-element.773) | copy-start | bytes 49156
  422.3 68.4 %copy-start.59 = (s32[4,256]{1,0:T(4,128)}, s32[4,256]{1,0:T(4,128)S(1)}, u32[]{:S(2)}) copy-start(s32[4,256]{1,0:T(4,128)S(1)} %get-tuple-element.917) | copy-start | bytes 12292
  426.1 195.6 %copy-start.5 = (f32[256,1024]{1,0:T(8,128)}, f32[256,1024]{1,0:T(8,128)S(1)}, u32[]{:S(2)}) copy-start(f32[256,1024]{1,0:T(8,128)S(1)} %get-tuple-element.451) | copy-start | bytes 3145732
  426.1 195.6 %copy-start.62 = (f32[256]{0:T(256)}, f32[256]{0:T(256)S(1)}, u32[]{:S(2)}) copy-start(f32[256]{0:T(256)S(1)} %broadcast_multiply_fusion.9) | copy-start | bytes 3076
  426.4 195.3 %copy-start.64 = (f32[256]{0:T(256)}, f32[256]{0:T(256)S(1)}, u32[]{:S(2)}) copy-start(f32[256]{0:T(256)S(1)} %add_rsqrt_fusion.1) | copy-start | bytes 3076
  553.2 7.1 copy-start.86
  553.2 20.5 %slice-start = ((s8[8388608]{0:T(1024)(128)(4,1)}), s8[4194304]{0:T(1024)(128)(4,1)S(1)}, s32[]{:S(2)}) async-start(s8[8388608]{0:T(1024)(128)(4,1)} %bitcast.494), calls=%async_computation.30 | async-start | bytes 8388608
  560.3 13.4 slice-start.1
  580.6 13.1 copy-start.44
  580.6 32.4 %copy-start.47 = (f32[256,1024]{1,0:T(8,128)}, f32[256,1024]{1,0:T(8,128)S(1)}, u32[]{:S(2)}) copy-start(f32[256,1024]{1,0:T(8,128)S(1)} %get-tuple-element.413) | copy-start | bytes 3145732
  580.6 13.1 copy-start.14
  593.7 7.5 copy-start.52
  613.0 8.7 copy-start.51
  613.0 10.6 copy-start.4
  625.4 7.1 copy-start.3
  625.4 7.1 copy-start.12
  678.2 4.1 copy-start.1
  678.2 4.1 copy-start.11
  678.2 84.1 %reduce-scatter.21.cloned.1.call-start = ((), (), s32[]{:S(2)}) async-start(), calls=%async_computation.18 | async-start | bytes 2621440 | tf_op jit(solution)/shard_map/reduce_scatter | solution.py:277
  728.2 72.3 %reduce-scatter.19.cloned.1.call-start = ((), (), s32[]{:S(2)}) async-start(), calls=%async_computation.17 | async-start | bytes 2621440 | tf_op jit(solution)/shard_map/reduce_scatter | solution.py:280
  728.9 109.9 %reduce-scatter.23.cloned.1.call-start = ((), (), s32[]{:S(2)}) async-start(), calls=%async_computation.19 | async-start | bytes 2621440 | tf_op jit(solution)/shard_map/reduce_scatter | solution.py:280
  729.5 254.8 %reduce-scatter.31.cloned.1.call-start = ((), (), s32[]{:S(2)}) async-start(), calls=%async_computation.27 | async-start | bytes 4325376
  738.8 387.8 %reduce-scatter.25.cloned.1.call-start = ((), (), s32[]{:S(2)}) async-start(), calls=%async_computation.24 | async-start | bytes 4325376 | tf_op jit(solution)/shard_map/reduce_scatter | solution.py:309
  743.9 524.5 %reduce-scatter.33.cloned.1.call-start = ((), (), s32[]{:S(2)}) async-start(), calls=%async_computation.28 | async-start | bytes 4325376
  772.7 637.9 %reduce-scatter.35.cloned.1.call-start = ((), (), s32[]{:S(2)}) async-start(), calls=%async_computation.29 | async-start | bytes 4325376
  849.2 5.1 copy-start.6
  849.2 5.1 copy-start.63
  849.2 5.1 copy-start.65
  849.3 747.7 %reduce-scatter.27.cloned.1.call-start = ((), (), s32[]{:S(2)}) async-start(), calls=%async_computation.25 | async-start | bytes 17301504 | tf_op jit(solution)/shard_map/reduce_scatter | solution.py:313
  864.3 919.8 %reduce-scatter.29.cloned.1.call-start = ((), (), s32[]{:S(2)}) async-start(), calls=%async_computation.26 | async-start | bytes 17301504 | tf_op jit(solution)/shard_map/reduce_scatter | solution.py:315
  879.6 3.8 copy-start.72
  879.7 4.4 copy-start.66
  879.7 4.3 copy-start.67
  881.0 9.3 copy-start.17
  881.6 8.7 copy-start.26
  886.9 5.2 copy-start.35
  886.9 5.4 copy-start.38
  890.4 51.1 %copy-start.39 = (bf16[1,256,1024]{1,2,0:T(8,128)(2,1)S(1)}, bf16[1,256,1024]{1,2,0:T(8,128)(2,1)}, u32[]{:S(2)}) copy-start(bf16[1,256,1024]{1,2,0:T(8,128)(2,1)} %reduce-scatter.23.cloned.1.call-done) | copy-start | bytes 1572868
  892.1 49.3 %copy-start.23 = (bf16[1024,1024]{1,0:T(8,128)(2,1)S(1)}, bf16[1024,1024]{1,0:T(8,128)(2,1)}, u32[]{:S(2)}) copy-start(bf16[1024,1024]{1,0:T(8,128)(2,1)} %all-gather.16.cloned.1.call-done) | copy-start | bytes 6291460
  938.5 3.8 copy-start.46
  938.5 3.8 copy-start.48
  (87 other events, 177.3 us)
Sparse Core Ops, SparseCore 0:
  11.0 59.1 all-gather.15
  73.2 55.4 all-gather.19
  131.7 55.3 all-gather.17
  189.4 34.2 all-gather.27
  225.9 35.2 all-gather.29
  263.0 35.2 all-gather.31
  300.2 35.2 all-gather.33
  338.5 56.4 all-gather.21
  398.0 76.2 all-gather.23
  477.1 76.0 all-gather.25
  678.3 33.7 reduce-scatter.16
  728.3 33.9 reduce-scatter.20
  765.3 35.1 reduce-scatter.18
  803.6 35.1 reduce-scatter.22
  841.5 142.7 reduce-scatter.30
  987.0 139.5 reduce-scatter.24
  1129.3 139.0 reduce-scatter.32
  1271.1 139.4 reduce-scatter.34
  1413.5 183.4 reduce-scatter.26
  1599.7 184.3 reduce-scatter.28
where the time goes:
time: 1800 us; the launch traced here: 1790 us
  waiting for transfers between devices  1260 us (70%)
  matrix products  253 us (14%)
  blocking collectives  122 us (7%)
  local copies, waits for them, and re-layouts  96.3 us (5%)
  other arithmetic  39.1 us (2%)
    unnamed x23, waiting for transfers between devices  328 us
    reduce_scatter x1, waiting for transfers between devices, body(): lax.psum_scatter(grad_down_mat, ('ctx', 'fsdp'), scatter_dimension=0, til...  187 us
    reduce_scatter x1, waiting for transfers between devices, body(): lax.psum_scatter(grad_up_mat, ('ctx', 'fsdp'), scatter_dimension=0, tiled...  186 us
    reduce_scatter x1, waiting for transfers between devices, body(): lax.psum_scatter(grad_out_mat, ('ctx', 'fsdp'), scatter_dimension=0, tile...  142 us
    unnamed x2, blocking collectives  82.9 us
    all_gather x2, waiting for transfers between devices, body(): lax.all_gather(keys_mine.reshape(per_device, ctx_rows, width), 'ctx', axi...  66.5 us
    all_gather x1, waiting for transfers between devices, body(): lax.all_gather(w_down, ('ctx', 'fsdp'), axis=0, tiled=True)  62.5 us
    reduce_scatter x2, waiting for transfers between devices, body(): lax.psum_scatter(grad_values_all.astype(jnp.bfloat16), 'ctx', scatter_dim...  62.4 us
  transfers between devices with their start and end apart: 20, of which 19 were waited for; matrix products, arithmetic and copies ran while one was open for 14% of the time, Pallas kernels for 0%

commit v1 on v0

--- a/solution.py
+++ b/solution.py
@@ -8,6 +8,18 @@
 EPSILON = 1e-12
 SCORE_SCALE = 0.125
 MASKED_SCORE = -1e30
+
+
+def doubled_up(array, axis, dim):
+    ways, here = (lax.axis_size(axis), lax.axis_index(axis))
+    grown, reach = (array, 1)
+    while reach < ways:
+        theirs = lax.ppermute(grown, axis, [(d, d ^ reach) for d in range(ways)])
+        mine_first = jnp.concatenate([grown, theirs], axis=dim)
+        theirs_first = jnp.concatenate([theirs, grown], axis=dim)
+        grown = jnp.where(here & reach == 0, mine_first, theirs_first)
+        reach = 2 * reach
+    return grown
 
 
 def exact_gelu(values_in):
@@ -140,7 +152,7 @@
             lax.all_gather(b_out, ("ctx", "fsdp"), axis=0, tiled=True),
             lax.all_gather(ln1_gain, ("ctx", "fsdp"), axis=0, tiled=True),
             lax.all_gather(ln1_bias, ("ctx", "fsdp"), axis=0, tiled=True),
-            lax.all_gather(w_up, ("ctx", "fsdp"), axis=0, tiled=True),
+            doubled_up(w_up, ("ctx", "fsdp"), 0),
             lax.all_gather(b_up, ("ctx", "fsdp"), axis=0, tiled=True),
             lax.all_gather(w_down, ("ctx", "fsdp"), axis=0, tiled=True),
             lax.all_gather(b_down, ("ctx", "fsdp"), axis=0, tiled=True),

time: 1800 us -> 1850 us (1.028)
  waiting for transfers between devices: 1260 us -> 1300 us
    ppermute x0 -> x5, waiting for transfers between devices: none -> 86.7 us  [doubled_up(): theirs = lax.ppermute(grown, axis, [(d, d ^ reach) for d in range(ways)])]
    all_gather x1, waiting for transfers between devices: 56.6 us -> 28.8 us  [body(): lax.all_gather(w_out, ('ctx', 'fsdp'), axis=0, tiled=True)]
    all_gather x1, waiting for transfers between devices: 62.5 us -> 42.5 us  [body(): lax.all_gather(w_down, ('ctx', 'fsdp'), axis=0, tiled=True)]
  transfers between devices with their start and end apart: 20 -> 25, of which waited for: 19 -> 21; matrix products, arithmetic and copies ran while one was open for 14% -> 16% of each run, Pallas kernels for 0% -> 0%
where the time goes in v1:
time: 1850 us; the launch traced here: 1840 us
  waiting for transfers between devices  1300 us (70%)
  matrix products  248 us (13%)
  blocking collectives  122 us (7%)
  local copies, waits for them, and re-layouts  98.7 us (5%)
  other arithmetic  48 us (3%)
    unnamed x23, waiting for transfers between devices  329 us
    reduce_scatter x1, waiting for transfers between devices, body(): lax.psum_scatter(grad_down_mat, ('ctx', 'fsdp'), scatter_dimension=0, til...  187 us
    reduce_scatter x1, waiting for transfers between devices, body(): lax.psum_scatter(grad_up_mat, ('ctx', 'fsdp'), scatter_dimension=0, tiled...  187 us
    reduce_scatter x1, waiting for transfers between devices, body(): lax.psum_scatter(grad_out_mat, ('ctx', 'fsdp'), scatter_dimension=0, tile...  142 us
    ppermute x5, waiting for transfers between devices, doubled_up(): theirs = lax.ppermute(grown, axis, [(d, d ^ reach) for d in range(ways)])  86.7 us
    unnamed x2, blocking collectives  82.8 us
    all_gather x2, waiting for transfers between devices, body(): lax.all_gather(keys_mine.reshape(per_device, ctx_rows, width), 'ctx', axi...  74.2 us
    reduce_scatter x2, waiting for transfers between devices, body(): lax.psum_scatter(grad_values_all.astype(jnp.bfloat16), 'ctx', scatter_dim...  62.4 us
  transfers between devices with their start and end apart: 25, of which 21 were waited for; matrix products, arithmetic and copies ran while one was open for 16% of the time, Pallas kernels for 0%

profile of v1, /device:TPU:0, one launch (start us, length us, event | category | flops | bytes accessed | tf_op | source)
XLA Modules:
  0.0 1841.5 jit_solution(10625134275948415095)
XLA Ops:
  16.2 42.3 %all-reduce.18 = (bf16[1024]{0:T(1024)(128)(2,1)S(1)}, bf16[1024]{0:T(1024)(128)(2,1)S(1)}, bf16[1024]{0:T(1024)(128)(2,1)S(1)}, bf16[1024]{0:T(1024)(128)(2,1)S...) all-reduce(bf16[1024]{0:T(1024)(128)(2,1)S(1)} %dynamic-update-slic, ...), channel_id=1, replica_groups=mesh['ctx'=4,'fsdp'=8] {'ctx','fsdp'}, use_global_device_ids=true, to_apply=%add | all-reduce | flops 8192 | bytes 32768
  58.5 11.8 all-gather.16.cloned.1.call-done
  70.2 3.4 fusion.134
  73.7 55.0 %all-gather.20.cloned.1.call-done = bf16[1024,1024]{1,0:T(8,128)(2,1)} async-done(((bf16[32,1024]{1,0:T(8,128)(2,1)}), bf16[1024,1024]{1,0:T(8,128)(2,1)}) %all-gather.20.cloned.1.call-update) | async-done | bytes 2097168 | tf_op jit(solution)/shard_map/all_gather | solution.py:148
  128.8 3.1 convolution_convert_fusion.3
  133.5 3.2 convolution_convert_fusion.2
  140.6 14.7 collective-permute-done.1
  156.8 49.4 %collective-permute-done.2 = bf16[128,4096]{1,0:T(8,128)(2,1)} collective-permute-done((bf16[128,4096]{1,0:T(8,128)(2,1)S(1)}, bf16[128,4096]{1,0:T(8,128)(2,1)}, u32[]{:S(2)}, u32[]{:S(2)}) %collective-permute-start.2) | collective-permute-done | bytes 1048608 | tf_op jit(solution)/shard_map/ppermute | solution.py:17
  206.2 3.0 maximum_select_fusion.2
  211.4 39.4 %all-gather.4 = bf16[32,1,128]{2,1,0:T(2,128)(2,1)S(1)} all-gather(bf16[1,1,128]{2,1,0:T(2,128)(2,1)S(1)} %bitcast.491), channel_id=1, replica_groups=mesh['ctx'=4,'fsdp'=8] {'ctx','fsdp'}, dimensions={0}, use_global_device_ids=true | all-gather | bytes 8448 | tf_op jit(solution)/shard_map/all_gather | solution.py:156
  252.6 21.4 %collective-permute-done.3 = bf16[256,4096]{1,0:T(8,128)(2,1)} collective-permute-done((bf16[256,4096]{1,0:T(8,128)(2,1)S(1)}, bf16[256,4096]{1,0:T(8,128)(2,1)}, u32[]{:S(2)}, u32[]{:S(2)}) %collective-permute-start.3) | collective-permute-done | bytes 2097184 | tf_op jit(solution)/shard_map/ppermute | solution.py:17
  274.0 4.7 maximum_select_fusion.1
  280.2 3.2 fusion.135
  289.1 3.9 copy.68
  293.0 38.0 %all-gather.30.cloned.1.call-done = bf16[1024,1024]{1,0:T(8,128)(2,1)} async-done(((bf16[256,1024]{1,0:T(8,128)(2,1)}), bf16[1024,1024]{1,0:T(8,128)(2,1)}) %all-gather.30.cloned.1.call-update) | async-done | bytes 2097168 | tf_op jit(solution)/shard_map/all_gather | solution.py:190
  331.0 2.9 copy.70
  334.7 26.7 %while.52 = (s32[]{:T(128)}, bf16[4,256,4,64]{1,3,2,0:T(8,128)(2,1)}, f32[4,4,256,1]{2,1,3,0:T(4,128)S(1)}, bf16[4,1024,4,64]{1,3,2,0:T(8,128)(2,1)}, s32[4,256]...) while((s32[]{:T(128)}, ...), condition=%wide.region_6.7_spmd, body=%wide.region_3.6_spmd.sunk | while | flops 281279488 | bytes 19317928 | solution.py:205
  361.5 23.7 %all-gather.32.cloned.1.call-done = bf16[1024,1024]{1,0:T(8,128)(2,1)} async-done(((bf16[256,1024]{1,0:T(8,128)(2,1)}), bf16[1024,1024]{1,0:T(8,128)(2,1)}) %all-gather.32.cloned.1.call-update) | async-done | bytes 2097168 | tf_op jit(solution)/shard_map/all_gather | solution.py:193
  385.2 4.0 copy.71
  389.1 36.2 %all-gather.34.cloned.1.call-done = bf16[1024,1024]{1,0:T(8,128)(2,1)} async-done(((bf16[256,1024]{1,0:T(8,128)(2,1)}), bf16[1024,1024]{1,0:T(8,128)(2,1)}) %all-gather.34.cloned.1.call-update) | async-done | bytes 2097168 | tf_op jit(solution)/shard_map/all_gather | solution.py:190
  425.3 2.9 copy.73
  429.1 26.9 %while.53 = (s32[]{:T(128)}, bf16[4,256,4,64]{1,3,2,0:T(8,128)(2,1)}, f32[4,4,256,1]{2,1,3,0:T(4,128)S(1)}, bf16[4,1024,4,64]{1,3,2,0:T(8,128)(2,1)}, s32[4,256]...) while((s32[]{:T(128)}, ...), condition=%wide.region_17.18_spmd, body=%wide.region_14.17_spmd.sunk | while | flops 281279488 | bytes 19317928 | solution.py:205
  456.0 28.8 %all-gather.22.cloned.1.call-done = bf16[1024,1024]{1,0:T(8,128)(2,1)} async-done(((bf16[32,1024]{1,0:T(8,128)(2,1)}), bf16[1024,1024]{1,0:T(8,128)(2,1)}) %all-gather.22.cloned.1.call-update) | async-done | bytes 2097168 | tf_op jit(solution)/shard_map/all_gather | solution.py:151
  489.0 16.2 multiply_convert_fusion.3
  505.3 16.3 multiply_convert_fusion.2
  521.6 42.5 %all-gather.24.cloned.1.call-done = bf16[4096,1024]{1,0:T(8,128)(2,1)} async-done(((bf16[128,1024]{1,0:T(8,128)(2,1)}), bf16[4096,1024]{1,0:T(8,128)(2,1)}) %all-gather.24.cloned.1.call-update) | async-done | bytes 8388624 | tf_op jit(solution)/shard_map/all_gather | solution.py:157
  564.1 6.8 fusion.214
  575.5 2.8 convert_reduce_fusion.4
  578.3 8.1 convert_reduce_fusion.1
  586.5 56.5 %all-gather.26.cloned.1.call-done = bf16[1024,4096]{1,0:T(8,128)(2,1)} async-done(((bf16[32,4096]{1,0:T(8,128)(2,1)}), bf16[1024,4096]{1,0:T(8,128)(2,1)}) %all-gather.26.cloned.1.call-update) | async-done | bytes 8388624 | tf_op jit(solution)/shard_map/all_gather | solution.py:230
  643.0 7.5 multiply_reduce_fusion.3
  650.5 11.6 convert_reduce_fusion
  662.1 8.6 convert_reduce_fusion.7
  674.4 2.8 convolution_convert_fusion.1
  681.4 45.9 %while.54 = (s32[]{:T(128)}, bf16[4,256,4,64]{1,3,2,0:T(8,128)(2,1)S(1)}, bf16[4,1024,4,64]{1,3,2,0:T(8,128)(2,1)}, bf16[4,1024,4,64]{1,3,2,0:T(8,128)(2,1)}, bf...) while((s32[]{:T(128)}, ...), condition=%wide.region_28.29_spmd, body=%wide.region_26.28_spmd.sunk | while | flops 687406080 | bytes 72663312 | solution.py:274
  684.7 2.8 multiply_reduce_fusion.14
  707.6 2.8 multiply_reduce_fusion.14
  719.0 2.8 multiply_reduce_fusion.14
  731.4 46.0 %while.55 = (s32[]{:T(128)}, bf16[4,256,4,64]{1,3,2,0:T(8,128)(2,1)}, bf16[4,1024,4,64]{1,3,2,0:T(8,128)(2,1)}, bf16[4,1024,4,64]{1,3,2,0:T(8,128)(2,1)}, bf16[4...) while((s32[]{:T(128)}, ...), condition=%wide.region_37.38_spmd, body=%wide.region_35.37_spmd.sunk | while | flops 687406080 | bytes 76857680 | solution.py:274
  746.0 2.8 multiply_reduce_fusion.15
  757.5 2.8 multiply_reduce_fusion.15
  782.6 5.8 copy.79
  793.7 3.7 fusion.157
  797.4 14.2 reduce-scatter.21.cloned.1.call-done
  811.5 5.0 add_bitcast_fusion.1
  816.6 5.3 copy.81
  822.0 27.8 %reduce-scatter.19.cloned.1.call-done = bf16[1,256,1024]{1,2,0:T(8,128)(2,1)} async-done(((bf16[1,1024,1024]{1,2,0:T(8,128)(2,1)}), bf16[1,256,1024]{1,2,0:T(8,128)(2,1)}) %reduce-scatter.19.cloned.1.call-update) | async-done | bytes 524304 | tf_op jit(solution)/shard_map/reduce_scatter | solution.py:292
  849.7 3.7 fusion.154
  853.4 34.6 %reduce-scatter.23.cloned.1.call-done = bf16[1,256,1024]{1,2,0:T(8,128)(2,1)} async-done(((bf16[1,1024,1024]{1,2,0:T(8,128)(2,1)}), bf16[1,256,1024]{1,2,0:T(8,128)(2,1)}) %reduce-scatter.23.cloned.1.call-update) | async-done | bytes 524304 | tf_op jit(solution)/shard_map/reduce_scatter | solution.py:292
  888.0 5.0 add_bitcast_fusion
  893.0 5.4 copy.83
  899.1 4.4 fusion.205
  903.6 10.0 convolution_add_fusion.1
  914.8 4.0 fusion.197
  918.8 10.1 convolution_add_fusion
  936.2 3.4 convolution_add_fusion.7
  941.9 40.5 %all-reduce.17 = (f32[1024]{0:T(1024)S(1)}, f32[1024]{0:T(1024)S(1)}, f32[1024]{0:T(1024)S(1)}, f32[1024]{0:T(1024)S(1)}, f32[1024]{0:T(1024)S(1)}, /*index=5*/f...) all-reduce(f32[1024]{0:T(1024)S(1)} %reshape.711, ...), channel_id=26, replica_groups=mesh['ctx'=4,'fsdp'=8] {'ctx','fsdp'}, use_global_device_ids=true, to_apply=%region_43.44.clone | all-reduce | flops 12288 | bytes 98304
  987.7 2.9 convolution_add_fusion.6
  994.5 39.2 %reduce-scatter.31.cloned.1.call-done = f32[32,1024]{1,0:T(8,128)} async-done(((f32[1024,1024]{1,0:T(8,128)}), f32[32,1024]{1,0:T(8,128)}) %reduce-scatter.31.cloned.1.call-update) | async-done | bytes 131088
  1033.8 142.1 %reduce-scatter.25.cloned.1.call-done = f32[32,1024]{1,0:T(8,128)} async-done(((f32[1024,1024]{1,0:T(8,128)}), f32[32,1024]{1,0:T(8,128)}) %reduce-scatter.25.cloned.1.call-update) | async-done | bytes 131088 | tf_op jit(solution)/shard_map/reduce_scatter | solution.py:321
  1175.8 142.6 %reduce-scatter.33.cloned.1.call-done = f32[32,1024]{1,0:T(8,128)} async-done(((f32[1024,1024]{1,0:T(8,128)}), f32[32,1024]{1,0:T(8,128)}) %reduce-scatter.33.cloned.1.call-update) | async-done | bytes 131088
  1318.4 142.0 %reduce-scatter.35.cloned.1.call-done = f32[32,1024]{1,0:T(8,128)} async-done(((f32[1024,1024]{1,0:T(8,128)}), f32[32,1024]{1,0:T(8,128)}) %reduce-scatter.35.cloned.1.call-update) | async-done | bytes 131088
  1460.4 187.0 %reduce-scatter.27.cloned.1.call-done = f32[32,4096]{1,0:T(8,128)} async-done(((f32[1024,4096]{1,0:T(8,128)}), f32[32,4096]{1,0:T(8,128)}) %reduce-scatter.27.cloned.1.call-update) | async-done | bytes 524304 | tf_op jit(solution)/shard_map/reduce_scatter | solution.py:325
  1647.4 187.1 %reduce-scatter.29.cloned.1.call-done = f32[128,1024]{1,0:T(8,128)} async-done(((f32[4096,1024]{1,0:T(8,128)}), f32[128,1024]{1,0:T(8,128)}) %reduce-scatter.29.cloned.1.call-update) | async-done | bytes 524304 | tf_op jit(solution)/shard_map/reduce_scatter | solution.py:327
  (583 shorter events, 210.1 us)
Async XLA Ops:
  7.2 121.6 %copy-start.8 = (bf16[2,1,256,1024]{3,2,1,0:T(8,128)(2,1)S(1)}, bf16[2,1,256,1024]{3,2,1,0:T(8,128)(2,1)}, u32[]{:S(2)}) copy-start(bf16[2,1,256,1024]{3,2,1,0:T(8,128)(2,1)} %param.26) | copy-start | bytes 3145732
  7.2 63.0 %all-gather.16.cloned.1.call-start = ((), (), s32[]{:S(2)}) async-start(), calls=%async_computation.10 | async-start | bytes 2162688 | tf_op jit(solution)/shard_map/all_gather | solution.py:149
  7.9 120.8 %all-gather.20.cloned.1.call-start = ((), (), s32[]{:S(2)}) async-start(), calls=%async_computation.12 | async-start | bytes 2162688 | tf_op jit(solution)/shard_map/all_gather | solution.py:148
  8.7 271.6 %all-gather.18.cloned.1.call-start = ((), (), s32[]{:S(2)}) async-start(), calls=%async_computation.11 | async-start | bytes 2162688 | tf_op jit(solution)/shard_map/all_gather | solution.py:146
  9.4 279.7 %all-gather.28.cloned.1.call-start = ((), (), s32[]{:S(2)}) async-start(), calls=%async_computation.20 | async-start | bytes 2621440 | tf_op jit(solution)/shard_map/all_gather | solution.py:193
  70.2 61.7 %copy-start.24 = (bf16[1024,1024]{1,0:T(8,128)(2,1)S(1)}, bf16[1024,1024]{1,0:T(8,128)(2,1)}, u32[]{:S(2)}) copy-start(bf16[1024,1024]{1,0:T(8,128)(2,1)} %all-gather.16.cloned.1.call-done) | copy-start | bytes 6291460
  73.7 257.3 %all-gather.30.cloned.1.call-start = ((), (), s32[]{:S(2)}) async-start(), calls=%async_computation.21 | async-start | bytes 2621440 | tf_op jit(solution)/shard_map/all_gather | solution.py:190
  131.9 6.4 copy-start.57
  131.9 253.2 %all-gather.32.cloned.1.call-start = ((), (), s32[]{:S(2)}) async-start(), calls=%async_computation.22 | async-start | bytes 2621440 | tf_op jit(solution)/shard_map/all_gather | solution.py:193
  133.5 291.8 %all-gather.34.cloned.1.call-start = ((), (), s32[]{:S(2)}) async-start(), calls=%async_computation.23 | async-start | bytes 2621440 | tf_op jit(solution)/shard_map/all_gather | solution.py:190
  136.7 74.7 %copy-start.91 = (bf16[128]{0:T(256)(128)(2,1)S(1)}, bf16[128]{0:T(256)(128)(2,1)}, u32[]{:S(2)}) copy-start(bf16[128]{0:T(256)(128)(2,1)} %param.38) | copy-start | bytes 772
  136.7 114.1 %copy-start.89 = (s32[2,1,4]{2,1,0:T(1,128)S(1)}, s32[2,1,4]{2,1,0:T(1,128)}, u32[]{:S(2)}) copy-start(s32[2,1,4]{2,1,0:T(1,128)} %param.27) | copy-start | bytes 100
  136.7 348.1 %all-gather.22.cloned.1.call-start = ((), (), s32[]{:S(2)}) async-start(), calls=%async_computation.13 | async-start | bytes 2162688 | tf_op jit(solution)/shard_map/all_gather | solution.py:151
  137.5 426.6 %all-gather.24.cloned.1.call-start = ((), (), s32[]{:S(2)}) async-start(), calls=%async_computation.14 | async-start | bytes 8650752 | tf_op jit(solution)/shard_map/all_gather | solution.py:157
  138.2 504.7 %all-gather.26.cloned.1.call-start = ((), (), s32[]{:S(2)}) async-start(), calls=%async_computation.15 | async-start | bytes 8650752 | tf_op jit(solution)/shard_map/all_gather | solution.py:230
  138.3 1.6 collective-permute-start
  140.0 15.3 collective-permute-start.1
  155.5 50.7 %collective-permute-start.2 = (bf16[128,4096]{1,0:T(8,128)(2,1)S(1)}, bf16[128,4096]{1,0:T(8,128)(2,1)}, u32[]{:S(2)}, u32[]{:S(2)}) collective-permute-start(bf16[128,4096]{1,0:T(8,128)(2,1)S(1)} %maximum_select_fusion.5), channel_id=1, source_target_pairs={{0,4},{1,5},{2,6},{3,7},{4,0},{5,1},{6,2},{7,3},{8,12},{9,13},{10,... | collective-permute-start | bytes 3145736 | tf_op jit(solution)/shard_map/ppermute | solution.py:17
  209.2 64.8 %collective-permute-start.3 = (bf16[256,4096]{1,0:T(8,128)(2,1)S(1)}, bf16[256,4096]{1,0:T(8,128)(2,1)}, u32[]{:S(2)}, u32[]{:S(2)}) collective-permute-start(bf16[256,4096]{1,0:T(8,128)(2,1)S(1)} %maximum_select_fusion.2), channel_id=1, source_target_pairs={{0,8},{1,9},{2,10},{3,11},{4,12},{5,13},{6,14},{7,15},{8,0},{9,1},... | collective-permute-start | bytes 6291464 | tf_op jit(solution)/shard_map/ppermute | solution.py:17
  210.7 582.9 %reduce-scatter.17.cloned.1.call-start = ((), (), s32[]{:S(2)}) async-start(), calls=%async_computation.16 | async-start | bytes 2621440 | tf_op jit(solution)/shard_map/reduce_scatter | solution.py:289
  251.2 320.0 %copy-start.58 = (f32[1024]{0:T(1024)}, f32[1024]{0:T(1024)S(1)}, u32[]{:S(2)}) copy-start(f32[1024]{0:T(1024)S(1)} %convert_element_type.386) | copy-start | bytes 12292
  278.7 210.3 %collective-permute-start.4 = (bf16[512,4096]{1,0:T(8,128)(2,1)}, bf16[512,4096]{1,0:T(8,128)(2,1)}, u32[]{:S(2)}, u32[]{:S(2)}) collective-permute-start(bf16[512,4096]{1,0:T(8,128)(2,1)} %maximum_select_fusion.1), channel_id=1, source_target_pairs={{0,16},{1,17},{2,18},{3,19},{4,20},{5,21},{6,22},{7,23},{8,24},{9,... | collective-permute-start | bytes 12582920 | tf_op jit(solution)/shard_map/ppermute | solution.py:17
  280.2 5.3 copy-start.27
  361.5 27.7 %copy-start.2 = (bf16[4,1024,4,64]{1,3,2,0:T(8,128)(2,1)}, bf16[4,1024,4,64]{1,3,2,0:T(8,128)(2,1)S(1)}, u32[]{:S(2)}) copy-start(bf16[4,1024,4,64]{1,3,2,0:T(8,128)(2,1)S(1)} %get-tuple-element.862) | copy-start | bytes 6291460
  361.5 66.7 %copy-start.61 = (s32[4,1024]{1,0:T(4,128)}, s32[4,1024]{1,0:T(4,128)S(1)}, u32[]{:S(2)}) copy-start(s32[4,1024]{1,0:T(4,128)S(1)} %get-tuple-element.914) | copy-start | bytes 49156
  361.5 66.7 %copy-start.62 = (f32[4,4,256,1]{2,1,3,0:T(4,128)}, f32[4,4,256,1]{2,1,3,0:T(4,128)S(1)}, u32[]{:S(2)}) copy-start(f32[4,4,256,1]{2,1,3,0:T(4,128)S(1)} %get-tuple-element.809) | copy-start | bytes 49156
  361.5 66.7 %copy-start.65 = (s32[4,256]{1,0:T(4,128)}, s32[4,256]{1,0:T(4,128)S(1)}, u32[]{:S(2)}) copy-start(s32[4,256]{1,0:T(4,128)S(1)} %get-tuple-element.924) | copy-start | bytes 12292
  456.0 32.7 %copy-start = (bf16[4,1024,4,64]{1,3,2,0:T(8,128)(2,1)}, bf16[4,1024,4,64]{1,3,2,0:T(8,128)(2,1)S(1)}, u32[]{:S(2)}) copy-start(bf16[4,1024,4,64]{1,3,2,0:T(8,128)(2,1)S(1)} %get-tuple-element.861) | copy-start | bytes 6291460
  456.0 32.7 %copy-start.60 = (s32[4,1024]{1,0:T(4,128)}, s32[4,1024]{1,0:T(4,128)S(1)}, u32[]{:S(2)}) copy-start(s32[4,1024]{1,0:T(4,128)S(1)} %get-tuple-element.913) | copy-start | bytes 49156
  456.0 32.7 %copy-start.63 = (f32[4,4,256,1]{2,1,3,0:T(4,128)}, f32[4,4,256,1]{2,1,3,0:T(4,128)S(1)}, u32[]{:S(2)}) copy-start(f32[4,4,256,1]{2,1,3,0:T(4,128)S(1)} %get-tuple-element.773) | copy-start | bytes 49156
  456.0 32.7 %copy-start.64 = (s32[4,256]{1,0:T(4,128)}, s32[4,256]{1,0:T(4,128)S(1)}, u32[]{:S(2)}) copy-start(s32[4,256]{1,0:T(4,128)S(1)} %get-tuple-element.923) | copy-start | bytes 12292
  487.5 17.7 copy-start.15
  488.7 181.9 %copy-start.6 = (f32[256,1024]{1,0:T(8,128)}, f32[256,1024]{1,0:T(8,128)S(1)}, u32[]{:S(2)}) copy-start(f32[256,1024]{1,0:T(8,128)S(1)} %get-tuple-element.451) | copy-start | bytes 3145732
  488.7 181.9 %copy-start.67 = (f32[256]{0:T(256)}, f32[256]{0:T(256)S(1)}, u32[]{:S(2)}) copy-start(f32[256]{0:T(256)S(1)} %broadcast_multiply_fusion.9) | copy-start | bytes 3076
  489.0 181.7 %copy-start.69 = (f32[256]{0:T(256)}, f32[256]{0:T(256)S(1)}, u32[]{:S(2)}) copy-start(f32[256]{0:T(256)S(1)} %add_rsqrt_fusion.1) | copy-start | bytes 3076
  505.3 58.8 %copy-start.90 = (f32[1024]{0:T(1024)S(1)}, f32[1024]{0:T(1024)}, u32[]{:S(2)}) copy-start(f32[1024]{0:T(1024)} %convert_element_type.390) | copy-start | bytes 12292
  521.6 49.6 %copy-start.39 = (bf16[256,4096]{1,0:T(8,128)(2,1)}, bf16[256,4096]{1,0:T(8,128)(2,1)S(1)}, u32[]{:S(2)}) copy-start(bf16[256,4096]{1,0:T(8,128)(2,1)S(1)} %get-tuple-element.422) | copy-start | bytes 6291460
  564.1 7.1 copy-start.92
  578.3 64.6 %copy-start.49 = (f32[256,1024]{1,0:T(8,128)}, f32[256,1024]{1,0:T(8,128)S(1)}, u32[]{:S(2)}) copy-start(f32[256,1024]{1,0:T(8,128)S(1)} %get-tuple-element.436) | copy-start | bytes 3145732
  578.3 64.6 %copy-start.16 = (f32[256,1024]{1,0:T(8,128)S(1)}, f32[256,1024]{1,0:T(8,128)}, u32[]{:S(2)}) copy-start(f32[256,1024]{1,0:T(8,128)} %copy-done.15) | copy-start | bytes 3145732
  643.0 7.5 copy-start.52
  643.0 7.5 copy-start.93
  662.1 8.6 copy-start.56
  662.1 10.5 copy-start.5
  674.4 7.1 copy-start.3
  674.4 7.1 copy-start.14
  727.3 84.2 %reduce-scatter.21.cloned.1.call-start = ((), (), s32[]{:S(2)}) async-start(), calls=%async_computation.18 | async-start | bytes 2621440 | tf_op jit(solution)/shard_map/reduce_scatter | solution.py:289
  777.5 72.3 %reduce-scatter.19.cloned.1.call-start = ((), (), s32[]{:S(2)}) async-start(), calls=%async_computation.17 | async-start | bytes 2621440 | tf_op jit(solution)/shard_map/reduce_scatter | solution.py:292
  778.2 109.8 %reduce-scatter.23.cloned.1.call-start = ((), (), s32[]{:S(2)}) async-start(), calls=%async_computation.19 | async-start | bytes 2621440 | tf_op jit(solution)/shard_map/reduce_scatter | solution.py:292
  778.8 255.0 %reduce-scatter.31.cloned.1.call-start = ((), (), s32[]{:S(2)}) async-start(), calls=%async_computation.27 | async-start | bytes 4325376
  788.4 387.4 %reduce-scatter.25.cloned.1.call-start = ((), (), s32[]{:S(2)}) async-start(), calls=%async_computation.24 | async-start | bytes 4325376 | tf_op jit(solution)/shard_map/reduce_scatter | solution.py:321
  793.6 524.8 %reduce-scatter.33.cloned.1.call-start = ((), (), s32[]{:S(2)}) async-start(), calls=%async_computation.28 | async-start | bytes 4325376
  821.9 638.5 %reduce-scatter.35.cloned.1.call-start = ((), (), s32[]{:S(2)}) async-start(), calls=%async_computation.29 | async-start | bytes 4325376
  898.5 5.1 copy-start.7
  898.5 5.1 copy-start.68
  898.5 5.1 copy-start.70
  898.5 748.9 %reduce-scatter.27.cloned.1.call-start = ((), (), s32[]{:S(2)}) async-start(), calls=%async_computation.25 | async-start | bytes 17301504 | tf_op jit(solution)/shard_map/reduce_scatter | solution.py:325
  913.6 920.9 %reduce-scatter.29.cloned.1.call-start = ((), (), s32[]{:S(2)}) async-start(), calls=%async_computation.26 | async-start | bytes 17301504 | tf_op jit(solution)/shard_map/reduce_scatter | solution.py:327
  930.3 9.3 copy-start.19
  930.9 8.7 copy-start.28
  936.1 5.2 copy-start.37
  936.2 5.5 copy-start.40
  939.6 51.0 %copy-start.41 = (bf16[1,256,1024]{1,2,0:T(8,128)(2,1)S(1)}, bf16[1,256,1024]{1,2,0:T(8,128)(2,1)}, u32[]{:S(2)}) copy-start(bf16[1,256,1024]{1,2,0:T(8,128)(2,1)} %reduce-scatter.23.cloned.1.call-done) | copy-start | bytes 1572868
  941.4 49.3 %copy-start.25 = (bf16[1024,1024]{1,0:T(8,128)(2,1)S(1)}, bf16[1024,1024]{1,0:T(8,128)(2,1)}, u32[]{:S(2)}) copy-start(bf16[1024,1024]{1,0:T(8,128)(2,1)} %all-gather.16.cloned.1.call-done) | copy-start | bytes 6291460
  (103 other events, 227.7 us)
Sparse Core Ops, SparseCore 0:
  11.0 59.1 all-gather.15
  73.2 55.4 all-gather.19
  131.7 97.1 all-gather.17
  231.2 46.5 all-gather.27
  279.4 51.5 all-gather.29
  332.7 52.3 all-gather.31
  387.0 38.2 all-gather.33
  428.3 56.4 all-gather.21
  487.8 76.2 all-gather.23
  566.9 75.9 all-gather.25
  727.5 33.7 reduce-scatter.16
  777.6 33.9 reduce-scatter.20
  814.5 35.1 reduce-scatter.18
  852.8 35.1 reduce-scatter.22
  890.7 142.9 reduce-scatter.30
  1036.5 139.3 reduce-scatter.24
  1178.5 139.8 reduce-scatter.32
  1321.1 139.2 reduce-scatter.34
  1463.2 184.0 reduce-scatter.26
  1650.1 184.3 reduce-scatter.28
